TPU v7x, 32 devices: a whole 2x2x4 slice. The times are simulated.
32 devices in a mesh: date: 2 (over y), trade: 8 (over z, x), path: 2 (over core).
Axes of the slice: x: 2, y: 2, z: 4, core: 2. Of those that a mesh axis runs over, the one named last changes fastest.
Arguments:
- basis_values: bfloat16 [2048, 512], P(('date', 'path')), parts along dimension 0, may hold values from -6 to 6
- coefficients: bfloat16 [2560, 512], P(('date', 'trade')), parts along dimension 0, may hold values from -0.25 to 0.25
- trade_cpty: int32 [1280], P('trade'), may hold values from 0 to 127, as said below
- trade_bucket: int32 [1280], P('trade'), may hold values from 0 to 127
- risk_weights: float32 [128], replicated, may hold values from 0.5 to 2
- correlation: float32 [128, 128], replicated, may hold values from 0 to 1, as said below
- funding_spread: float32 [128], P('trade'), may hold values from 0.5 to 2
Outputs:
- margin: float32 [128, 2048], P('trade', ('date', 'path')), parts along dimension 1
- basis_adjoint: bfloat16 [2048, 512], P(('date', 'path')), parts along dimension 0
There are 2 independent parts, one for each index of `date`. A program takes and returns all parts, laid end to end along the dimension named above; an argument that names none is the same for every part. Nothing has to cross between parts.
Inputs may be any that keep to these rules, and one draw needn't show every extreme that they name: `trade_cpty`: counterparty c belongs to owner block c // 16. Among the trades of one device, at most 40 belong to counterparties of one owner block; in every draw one owner block receives exactly 40 from every device. Counterparties differ in size. `correlation`: symmetric positive definite with unit diagonal; smallest eigenvalue at least 0.01; entries positive.
All inputs are finite; a program needn't handle non-finite values.
Results may differ from a plain program's by a relative error of at most 0.0034.
Values may be sent and summed in bfloat16 or wider, within the bound.
No kernel may reach another device: no remote copies, remote signals or barrier semaphores. Data moves between devices by JAX's collectives and lax.ppermute only.
A program may use at most 64 MiB of HBM per device.

v0:
```python
import jax
import jax.numpy as jnp
from jax import lax
from jax.sharding import PartitionSpec as P


def margin_terms(arrived, got_codes, risk_weights, correlation, funding_spread):
    path_rows = arrived.shape[0]
    cpty_count = funding_spread.shape[0]
    bucket_count = risk_weights.shape[0]
    is_filled = got_codes >= 0
    column_ids = jnp.arange(cpty_count * bucket_count, dtype=jnp.int32)
    hot_table = (got_codes[:, None] == column_ids[None, :]).astype(jnp.bfloat16)
    bucket_sums = jnp.dot(arrived, hot_table, preferred_element_type=jnp.float32)
    weighted = (
        bucket_sums.reshape(path_rows, cpty_count, bucket_count) * risk_weights[None, None, :]
    )
    rho_w = jnp.einsum("pcb,db->pcd", weighted, correlation, precision=lax.Precision.HIGHEST)
    margin_now = jnp.sqrt(jnp.sum(weighted * rho_w, axis=2) + 1e-06)
    sens_bar = (
        funding_spread[None, :, None] * risk_weights[None, None, :] * rho_w / margin_now[:, :, None]
    )
    flat_bar = sens_bar.reshape(path_rows, cpty_count * bucket_count)
    safe_codes = jnp.where(is_filled, got_codes, 0)
    slot_bar = jnp.take(flat_bar, safe_codes, axis=1) * is_filled[None, :].astype(jnp.float32)
    return (margin_now, slot_bar.astype(jnp.bfloat16))


def body(
    basis_values, coefficients, trade_cpty, trade_bucket, risk_weights, correlation, funding_spread
):
    owners = lax.axis_size("trade")
    per_device = coefficients.shape[0]
    capacity = max(2, 2 * per_device // owners)
    slot_total = owners * capacity
    cpty_count = funding_spread.shape[0]
    bucket_count = risk_weights.shape[0]
    path_rows = basis_values.shape[0]
    owner_of = trade_cpty // cpty_count
    trade_code = trade_cpty % cpty_count * bucket_count + trade_bucket
    position = jnp.arange(per_device, dtype=jnp.int32)
    same_owner = owner_of[:, None] == owner_of[None, :]
    earlier = position[None, :] < position[:, None]
    rank_in = jnp.sum((same_owner & earlier).astype(jnp.int32), axis=1)
    slot_index = owner_of * capacity + rank_in
    codes_out = jnp.full((slot_total,), -1, jnp.int32).at[slot_index].set(trade_code)
    got_codes = lax.all_to_all(codes_out, "trade", split_axis=0, concat_axis=0, tiled=True)
    delta_rows = lax.dot_general(
        basis_values, coefficients, (((1,), (1,)), ((), ())), preferred_element_type=jnp.float32
    ).astype(jnp.bfloat16)
    outgoing = jnp.zeros((path_rows, slot_total), jnp.bfloat16).at[:, slot_index].set(delta_rows)
    arrived = lax.all_to_all(outgoing, "trade", split_axis=1, concat_axis=1, tiled=True)
    margin_now, slot_bar = margin_terms(
        arrived, got_codes, risk_weights, correlation, funding_spread
    )
    returned = lax.all_to_all(slot_bar, "trade", split_axis=1, concat_axis=1, tiled=True)
    delta_bar = returned[:, slot_index]
    partial_adj = jnp.dot(delta_bar, coefficients, preferred_element_type=jnp.float32)
    basis_adjoint = lax.psum(partial_adj, "trade").astype(jnp.bfloat16)
    return (margin_now.T, basis_adjoint)


def solution(mesh):
    placed = (
        P(("date", "path"), None),
        P(("date", "trade"), None),
        P("trade"),
        P("trade"),
        P(),
        P(),
        P("trade"),
    )
    return jax.shard_map(
        body,
        mesh=mesh,
        in_specs=placed,
        out_specs=(P("trade", ("date", "path")), P(("date", "path"), None)),
        check_vma=False,
    )
```

profile of v0, /device:TPU:0, one launch (start us, length us, event | category | flops | bytes accessed | tf_op | source)
XLA Modules:
  0.0 130.3 jit_solution(14144373721821639996)
XLA Ops:
  0.6 0.0 copy-start
  0.6 0.8 fusion.14
  1.4 0.2 convert_reduce_fusion
  1.6 1.1 scatter_custom_fusion.1
  2.7 0.7 all_to_all.25
  3.4 7.3 %all-to-all-start.1 = ((s32[8,40,1]{1,2,0:T(1,128)}), s32[8,40,1]{1,2,0:T(1,128)S(1)}, u32[]{:S(2)}, u32[]{:S(2)}) async-start(s32[8,40,1]{1,2,0:T(1,128)} %all_to_all.25), calls=%async_computation.1 | async-start | bytes 8192 | tf_op jit(solution)/shard_map/all_to_all | solution.py:47
  10.6 0.0 copy-done
  10.7 1.2 fusion.7
  11.9 0.0 copy-start.2
  11.9 0.0 copy-start.3
  11.9 1.9 %scatter_custom_fusion = bf16[512,320]{0,1:T(8,128)(2,1)} fusion(s32[160]{0:T(256)S(1)} %compare_select_fusion.4, bf16[160,512]{1,0:T(8,128)(2,1)S(1)} %fusion.7, bf16[]{:T(256)} %constant.45.clone.1), kind=kCustom, calls=%fused_computation.18 | custom fusion | bytes 327682 | tf_op jit(solution)/shard_map/scatter | solution.py:51
  13.8 3.2 %all-to-all-done.1 = s32[8,40,1]{1,2,0:T(1,128)S(1)} async-done(((s32[8,40,1]{1,2,0:T(1,128)}), s32[8,40,1]{1,2,0:T(1,128)S(1)}, u32[]{:S(2)}, u32[]{:S(2)}) %all-to-all-start.1) | async-done | bytes 1312 | tf_op jit(solution)/shard_map/all_to_all | solution.py:47
  17.0 3.4 %all-to-all-start = ((bf16[512,8,40]{0,2,1:T(8,128)(2,1)}), bf16[512,8,40]{0,2,1:T(8,128)(2,1)S(1)}, u32[]{:S(2)}, u32[]{:S(2)}) async-start(bf16[512,8,40]{0,2,1:T(8,128)(2,1)} %bitcast.1), calls=%async_computation | async-start | bytes 655360 | tf_op jit(solution)/shard_map/all_to_all | solution.py:52
  20.5 0.7 broadcast_multiply_fusion
  21.2 0.5 broadcast.164
  21.7 0.7 reduce.7
  22.4 0.1 eq.51
  22.5 0.1 all_to_all.27
  22.6 6.9 %all-to-all-done = bf16[512,8,40]{0,2,1:T(8,128)(2,1)S(1)} async-done(((bf16[512,8,40]{0,2,1:T(8,128)(2,1)}), bf16[512,8,40]{0,2,1:T(8,128)(2,1)S(1)}, u32[]{:S(2)}, u32[]{:S(2)}) %all-to-all-start) | async-done | bytes 327712 | tf_op jit(solution)/shard_map/all_to_all | solution.py:52
  29.6 1.4 %fusion.2 = f32[512,16,128]{0,2,1:T(8,128)S(1)} fusion(bf16[512,320,1]{0,1,2:T(8,128)(2,1)S(1)} %bitcast.29, s32[16,128]{1,0:T(8,128)S(1)} %multiply_add_fusion, s32[320]{0:T(512)S(1)} %eq.51), kind=kOutput, calls=%fused_computation.8 | convolution fusion | flops 671744000 | bytes 4531456 | tf_op jit(solution)/shard_map/dot_general | solution.py:14
  30.9 0.0 copy-done.2
  30.9 0.0 copy-done.3
  31.0 5.5 %multiply_reduce_fusion = (f32[512,16]{0,1:T(8,128)S(1)}, f32[512,16,128]{0,2,1:T(8,128)S(1)}) fusion(f32[512,16,128]{0,2,1:T(8,128)S(1)} %fusion.2, f32[128]{0:T(128)S(1)} %copy-done.3, f32[128,128]{1,0:T(8,128)S(1)} %copy-done.2), kind=kOutput, calls=%fused_computation.5 | convolution fusion | flops 1614798848 | bytes 8487424 | tf_op jit(solution)/shard_map/pcb,db->pcd/dot_general | solution.py:18
  36.4 0.6 add_sqrt_fusion
  37.1 2.4 %multiply_divide_fusion = f32[512,16,128]{0,2,1:T(8,128)} fusion(f32[512,16,128]{0,2,1:T(8,128)S(1)} %get-tuple-element.9, f32[512,16]{0,1:T(8,128)S(1)} %get-tuple-element.2, f32[16,128]{1,0:T(8,128)S(1)} %broadcast_multiply_fusion), kind=kLoop, calls=%fused_computation.4 | loop fusion | flops 2097152 | bytes 8429568 | tf_op jit(solution)/shard_map/div | solution.py:21
  39.5 4.3 %gather_fusion = f32[320,512]{1,0:T(8,128)S(1)} fusion(f32[512,2048]{0,1:T(8,128)} %bitcast.26, s32[1024]{0:T(1024)S(1)} %pad_clamp_fusion.1), kind=kCustom, calls=%fused_computation | custom fusion | bytes 1312000 | tf_op jit(solution)/shard_map/jit(_take)/gather | solution.py:25
  43.8 0.9 multiply_convert_fusion
  44.7 3.6 %all-to-all-start.2 = ((bf16[512,8,40]{0,2,1:T(8,128)(2,1)}), bf16[512,8,40]{0,2,1:T(8,128)(2,1)S(1)}, u32[]{:S(2)}, u32[]{:S(2)}) async-start(bf16[512,8,40]{0,2,1:T(8,128)(2,1)} %multiply_convert_fusion), calls=%async_computation.2 | async-start | bytes 655360 | tf_op jit(solution)/shard_map/all_to_all | solution.py:56
  48.3 9.6 %all-to-all-done.2 = bf16[512,8,40]{0,2,1:T(8,128)(2,1)S(1)} async-done(((bf16[512,8,40]{0,2,1:T(8,128)(2,1)}), bf16[512,8,40]{0,2,1:T(8,128)(2,1)S(1)}, u32[]{:S(2)}, u32[]{:S(2)}) %all-to-all-start.2) | async-done | bytes 327712 | tf_op jit(solution)/shard_map/all_to_all | solution.py:56
  57.9 0.9 gather_fusion.1
  58.8 0.3 fusion.18
  59.2 71.2 %all-reduce.1 = bf16[512,512]{1,0:T(8,128)(2,1)} all-reduce(f32[512,512]{1,0:T(8,128)S(1)} %fusion.18), channel_id=1, replica_groups=mesh['date'=2,'trade'=8,'path'=2] {'trade'}, use_global_device_ids=true, to_apply=%region_4.5 | all-reduce | flops 262144 | bytes 1572864 | tf_op jit(solution)/shard_map/psum | solution.py:59
  (8 shorter events, 0.1 us)
Async XLA Ops:
  0.6 10.0 %copy-start = (bf16[512,512]{1,0:T(8,128)(2,1)S(1)}, bf16[512,512]{1,0:T(8,128)(2,1)}, u32[]{:S(2)}) copy-start(bf16[512,512]{1,0:T(8,128)(2,1)} %param.7) | copy-start | bytes 1572868
  3.4 13.6 %all-to-all-start.1 = ((s32[8,40,1]{1,2,0:T(1,128)}), s32[8,40,1]{1,2,0:T(1,128)S(1)}, u32[]{:S(2)}, u32[]{:S(2)}) async-start(s32[8,40,1]{1,2,0:T(1,128)} %all_to_all.25), calls=%async_computation.1 | async-start | bytes 8192 | tf_op jit(solution)/shard_map/all_to_all | solution.py:47
  11.9 19.0 %copy-start.2 = (f32[128,128]{1,0:T(8,128)S(1)}, f32[128,128]{1,0:T(8,128)}, u32[]{:S(2)}) copy-start(f32[128,128]{1,0:T(8,128)} %param.12) | copy-start | bytes 196612
  11.9 19.0 %copy-start.3 = (f32[128]{0:T(128)S(1)}, f32[128]{0:T(128)}, u32[]{:S(2)}) copy-start(f32[128]{0:T(128)} %param.11) | copy-start | bytes 1540
  17.0 12.5 %all-to-all-start = ((bf16[512,8,40]{0,2,1:T(8,128)(2,1)}), bf16[512,8,40]{0,2,1:T(8,128)(2,1)S(1)}, u32[]{:S(2)}, u32[]{:S(2)}) async-start(bf16[512,8,40]{0,2,1:T(8,128)(2,1)} %bitcast.1), calls=%async_computation | async-start | bytes 655360 | tf_op jit(solution)/shard_map/all_to_all | solution.py:52
  39.5 19.3 %copy-start.1 = (bf16[160,512]{1,0:T(8,128)(2,1)S(1)}, bf16[160,512]{1,0:T(8,128)(2,1)}, u32[]{:S(2)}) copy-start(bf16[160,512]{1,0:T(8,128)(2,1)} %param.8) | copy-start | bytes 491524
  44.7 13.2 %all-to-all-start.2 = ((bf16[512,8,40]{0,2,1:T(8,128)(2,1)}), bf16[512,8,40]{0,2,1:T(8,128)(2,1)S(1)}, u32[]{:S(2)}, u32[]{:S(2)}) async-start(bf16[512,8,40]{0,2,1:T(8,128)(2,1)} %multiply_convert_fusion), calls=%async_computation.2 | async-start | bytes 655360 | tf_op jit(solution)/shard_map/all_to_all | solution.py:56
where the time goes:
time: 131 us; the launch traced here: 130 us
  blocking collectives  71.2 us (54%)
  waiting for transfers between devices  19.8 us (15%)
  starting transfers between devices  14.3 us (11%)
  local copies, waits for them, and re-layouts  9.56 us (7%)
  matrix products  8.42 us (6%)
  other arithmetic  6.37 us (5%)
    psum x1, blocking collectives, body(): basis_adjoint = lax.psum(partial_adj, 'trade').astype(jnp.bfloat16)  71.2 us
    all_to_all x1, waiting for transfers between devices, body(): lax.all_to_all(slot_bar, 'trade', split_axis=1, concat_axis=1, tiled=True)  9.6 us
    all_to_all x1, starting transfers between devices, body(): lax.all_to_all(codes_out, 'trade', split_axis=0, concat_axis=0, tiled=True)  7.25 us
    all_to_all x1, waiting for transfers between devices, body(): lax.all_to_all(outgoing, 'trade', split_axis=1, concat_axis=1, tiled=True)  6.93 us
    dot_general x1, matrix products, margin_terms(): jnp.einsum('pcb,db->pcd', weighted, correlation, precision=lax.Precision....  5.47 us
    gather x1, local copies, waits for them, and re-layouts, margin_terms(): jnp.take(flat_bar, safe_codes, axis=1)  4.27 us
    all_to_all x1, starting transfers between devices, body(): lax.all_to_all(slot_bar, 'trade', split_axis=1, concat_axis=1, tiled=True)  3.6 us
    all_to_all x1, starting transfers between devices, body(): lax.all_to_all(outgoing, 'trade', split_axis=1, concat_axis=1, tiled=True)  3.43 us
  transfers between devices with their start and end apart: 3, of which 3 were waited for; matrix products, arithmetic and copies ran while one was open for 4% of the time, Pallas kernels for 0%

commit v1 on v0

--- a/solution.py
+++ b/solution.py
@@ -2,6 +2,11 @@
 import jax.numpy as jnp
 from jax import lax
 from jax.sharding import PartitionSpec as P
+
+
+def pack_lanes(point):
+    prior = lax.all_gather(point, axis_name="trade").sum(axis=0)
+    return prior
 
 
 def margin_terms(arrived, got_codes, risk_weights, correlation, funding_spread):
@@ -56,7 +61,7 @@
     returned = lax.all_to_all(slot_bar, "trade", split_axis=1, concat_axis=1, tiled=True)
     delta_bar = returned[:, slot_index]
     partial_adj = jnp.dot(delta_bar, coefficients, preferred_element_type=jnp.float32)
-    basis_adjoint = lax.psum(partial_adj, "trade").astype(jnp.bfloat16)
+    basis_adjoint = pack_lanes(partial_adj).astype(jnp.bfloat16)
     return (margin_now.T, basis_adjoint)
 
 

time: 131 us -> 204 us (1.56)
  waiting for transfers between devices: 19.8 us -> 144 us
  blocking collectives: 71.2 us -> 0 us
  between operations: 0.77 us -> 14.2 us
  other arithmetic: 6.37 us -> 11.7 us
    all_gather x0 -> x1, waiting for transfers between devices: none -> 124 us  [pack_lanes(): prior = lax.all_gather(point, axis_name='trade').sum(axis=0)]
    psum x1 -> x0, blocking collectives: 71.2 us -> none  [body(): basis_adjoint = lax.psum(partial_adj, 'trade').astype(jnp.bfloat16)]
    reduce_sum x0 -> x1, other arithmetic: none -> 5.33 us  [pack_lanes(): prior = lax.all_gather(point, axis_name='trade').sum(axis=0)]
  transfers between devices with their start and end apart: 3 -> 4, of which waited for: 3 -> 4; matrix products, arithmetic and copies ran while one was open for 4% -> 3% of each run, Pallas kernels for 0% -> 0%
where the time goes in v1:
time: 204 us; the launch traced here: 203 us
  waiting for transfers between devices  144 us (71%)
  starting transfers between devices  14.3 us (7%)
  between operations  14.2 us (7%)
  other arithmetic  11.7 us (6%)
  local copies, waits for them, and re-layouts  9.56 us (5%)
  matrix products  9.48 us (5%)
    all_gather x1, waiting for transfers between devices, pack_lanes(): prior = lax.all_gather(point, axis_name='trade').sum(axis=0)  124 us
    all_to_all x1, waiting for transfers between devices, body(): lax.all_to_all(slot_bar, 'trade', split_axis=1, concat_axis=1, tiled=True)  9.56 us
    all_to_all x1, starting transfers between devices, body(): lax.all_to_all(codes_out, 'trade', split_axis=0, concat_axis=0, tiled=True)  7.25 us
    all_to_all x1, waiting for transfers between devices, body(): lax.all_to_all(outgoing, 'trade', split_axis=1, concat_axis=1, tiled=True)  6.93 us
    dot_general x1, matrix products, margin_terms(): jnp.einsum('pcb,db->pcd', weighted, correlation, precision=lax.Precision....  5.47 us
    reduce_sum x1, other arithmetic, pack_lanes(): prior = lax.all_gather(point, axis_name='trade').sum(axis=0)  5.33 us
    gather x1, local copies, waits for them, and re-layouts, margin_terms(): jnp.take(flat_bar, safe_codes, axis=1)  4.27 us
  transfers between devices with their start and end apart: 4, of which 4 were waited for; matrix products, arithmetic and copies ran while one was open for 3% of the time, Pallas kernels for 0%

profile of v1, /device:TPU:0, one launch (start us, length us, event | category | flops | bytes accessed | tf_op | source)
XLA Modules:
  0.0 203.1 jit_solution(15023512614674162897)
XLA Ops:
  7.2 0.0 copy-start
  7.2 0.8 fusion.14
  7.9 0.2 convert_reduce_fusion
  8.1 1.1 scatter_custom_fusion.1
  9.2 0.7 all_to_all.25
  9.9 7.3 %all-to-all-start.1 = ((s32[8,40,1]{1,2,0:T(1,128)}), s32[8,40,1]{1,2,0:T(1,128)S(1)}, u32[]{:S(2)}, u32[]{:S(2)}) async-start(s32[8,40,1]{1,2,0:T(1,128)} %all_to_all.25), calls=%async_computation.1 | async-start | bytes 8192 | tf_op jit(solution)/shard_map/all_to_all | solution.py:52
  17.2 1.2 fusion.7
  18.4 0.0 copy-start.2
  18.4 0.0 copy-start.3
  18.5 1.9 scatter_custom_fusion
  20.3 3.2 %all-to-all-done.1 = s32[8,40,1]{1,2,0:T(1,128)S(1)} async-done(((s32[8,40,1]{1,2,0:T(1,128)}), s32[8,40,1]{1,2,0:T(1,128)S(1)}, u32[]{:S(2)}, u32[]{:S(2)}) %all-to-all-start.1) | async-done | bytes 1312 | tf_op jit(solution)/shard_map/all_to_all | solution.py:52
  23.6 3.4 %all-to-all-start = ((bf16[512,8,40]{0,2,1:T(8,128)(2,1)}), bf16[512,8,40]{0,2,1:T(8,128)(2,1)S(1)}, u32[]{:S(2)}, u32[]{:S(2)}) async-start(bf16[512,8,40]{0,2,1:T(8,128)(2,1)} %bitcast.1), calls=%async_computation | async-start | bytes 655360 | tf_op jit(solution)/shard_map/all_to_all | solution.py:57
  27.0 0.7 broadcast_multiply_fusion
  27.8 0.1 all_to_all.27
  27.8 0.5 broadcast.164
  28.4 0.7 reduce.7
  29.0 0.1 eq.51
  29.2 6.9 %all-to-all-done = bf16[512,8,40]{0,2,1:T(8,128)(2,1)S(1)} async-done(((bf16[512,8,40]{0,2,1:T(8,128)(2,1)}), bf16[512,8,40]{0,2,1:T(8,128)(2,1)S(1)}, u32[]{:S(2)}, u32[]{:S(2)}) %all-to-all-start) | async-done | bytes 327712 | tf_op jit(solution)/shard_map/all_to_all | solution.py:57
  36.1 1.4 fusion.2
  37.5 5.5 %multiply_reduce_fusion = (f32[512,16]{0,1:T(8,128)S(1)}, f32[512,16,128]{0,2,1:T(8,128)S(1)}) fusion(f32[512,16,128]{0,2,1:T(8,128)S(1)} %fusion.2, f32[128]{0:T(128)S(1)} %copy-done.3, f32[128,128]{1,0:T(8,128)S(1)} %copy-done.2), kind=kOutput, calls=%fused_computation.5 | convolution fusion | flops 1614798848 | bytes 8487424 | tf_op jit(solution)/shard_map/pcb,db->pcd/dot_general | solution.py:23
  43.0 0.6 add_sqrt_fusion
  43.6 2.4 %multiply_divide_fusion = f32[512,16,128]{0,2,1:T(8,128)} fusion(f32[512,16,128]{0,2,1:T(8,128)S(1)} %get-tuple-element.9, f32[512,16]{0,1:T(8,128)S(1)} %get-tuple-element.2, f32[16,128]{1,0:T(8,128)S(1)} %broadcast_multiply_fusion), kind=kLoop, calls=%fused_computation.4 | loop fusion | flops 2097152 | bytes 8429568 | tf_op jit(solution)/shard_map/div | solution.py:26
  46.0 4.3 %gather_fusion = f32[320,512]{1,0:T(8,128)S(1)} fusion(f32[512,2048]{0,1:T(8,128)} %bitcast.29, s32[1024]{0:T(1024)S(1)} %pad_clamp_fusion.1), kind=kCustom, calls=%fused_computation | custom fusion | bytes 1312000 | tf_op jit(solution)/shard_map/jit(_take)/gather | solution.py:30
  50.3 0.9 multiply_convert_fusion
  51.2 3.6 %all-to-all-start.2 = ((bf16[512,8,40]{0,2,1:T(8,128)(2,1)}), bf16[512,8,40]{0,2,1:T(8,128)(2,1)S(1)}, u32[]{:S(2)}, u32[]{:S(2)}) async-start(bf16[512,8,40]{0,2,1:T(8,128)(2,1)} %multiply_convert_fusion), calls=%async_computation.2 | async-start | bytes 655360 | tf_op jit(solution)/shard_map/all_to_all | solution.py:61
  54.8 0.0 all-gather.3.cloned.1.call-start
  54.9 9.6 %all-to-all-done.2 = bf16[512,8,40]{0,2,1:T(8,128)(2,1)S(1)} async-done(((bf16[512,8,40]{0,2,1:T(8,128)(2,1)}), bf16[512,8,40]{0,2,1:T(8,128)(2,1)S(1)}, u32[]{:S(2)}, u32[]{:S(2)}) %all-to-all-start.2) | async-done | bytes 327712 | tf_op jit(solution)/shard_map/all_to_all | solution.py:61
  64.4 0.9 gather_fusion.1
  65.3 1.4 fusion.18
  66.8 0.0 all-gather.3.cloned.1.call-update
  66.8 124.2 %all-gather.3.cloned.1.call-done = f32[4096,512]{1,0:T(8,128)} async-done(((f32[512,512]{1,0:T(8,128)}), f32[4096,512]{1,0:T(8,128)}) %all-gather.3.cloned.1.call-update) | async-done | bytes 8388624 | tf_op jit(solution)/shard_map/all_gather | solution.py:8
  191.0 5.3 %reduce_sum.29 = bf16[512,512]{1,0:T(8,128)(2,1)} reduce(f32[8,512,512]{2,1,0:T(8,128)} %bitcast.31, f32[]{:T(128)} %constant.55.clone.1), dimensions={0}, to_apply=%region_4.5 | reduce | flops 1835008 | bytes 8912900 | tf_op jit(solution)/shard_map/reduce_sum | solution.py:8
  (11 shorter events, 0.1 us)
Async XLA Ops:
  7.2 10.0 %copy-start = (bf16[512,512]{1,0:T(8,128)(2,1)S(1)}, bf16[512,512]{1,0:T(8,128)(2,1)}, u32[]{:S(2)}) copy-start(bf16[512,512]{1,0:T(8,128)(2,1)} %param.7) | copy-start | bytes 1572868
  9.9 13.6 %all-to-all-start.1 = ((s32[8,40,1]{1,2,0:T(1,128)}), s32[8,40,1]{1,2,0:T(1,128)S(1)}, u32[]{:S(2)}, u32[]{:S(2)}) async-start(s32[8,40,1]{1,2,0:T(1,128)} %all_to_all.25), calls=%async_computation.1 | async-start | bytes 8192 | tf_op jit(solution)/shard_map/all_to_all | solution.py:52
  18.4 19.0 %copy-start.2 = (f32[128,128]{1,0:T(8,128)S(1)}, f32[128,128]{1,0:T(8,128)}, u32[]{:S(2)}) copy-start(f32[128,128]{1,0:T(8,128)} %param.12) | copy-start | bytes 196612
  18.4 19.0 %copy-start.3 = (f32[128]{0:T(128)S(1)}, f32[128]{0:T(128)}, u32[]{:S(2)}) copy-start(f32[128]{0:T(128)} %param.11) | copy-start | bytes 1540
  23.6 12.5 %all-to-all-start = ((bf16[512,8,40]{0,2,1:T(8,128)(2,1)}), bf16[512,8,40]{0,2,1:T(8,128)(2,1)S(1)}, u32[]{:S(2)}, u32[]{:S(2)}) async-start(bf16[512,8,40]{0,2,1:T(8,128)(2,1)} %bitcast.1), calls=%async_computation | async-start | bytes 655360 | tf_op jit(solution)/shard_map/all_to_all | solution.py:57
  46.0 19.3 %copy-start.1 = (bf16[160,512]{1,0:T(8,128)(2,1)S(1)}, bf16[160,512]{1,0:T(8,128)(2,1)}, u32[]{:S(2)}) copy-start(bf16[160,512]{1,0:T(8,128)(2,1)} %param.8) | copy-start | bytes 491524
  51.2 13.2 %all-to-all-start.2 = ((bf16[512,8,40]{0,2,1:T(8,128)(2,1)}), bf16[512,8,40]{0,2,1:T(8,128)(2,1)S(1)}, u32[]{:S(2)}, u32[]{:S(2)}) async-start(bf16[512,8,40]{0,2,1:T(8,128)(2,1)} %multiply_convert_fusion), calls=%async_computation.2 | async-start | bytes 655360 | tf_op jit(solution)/shard_map/all_to_all | solution.py:61
  54.8 136.2 %all-gather.3.cloned.1.call-start = ((), (), s32[]{:S(2)}) async-start(), calls=%async_computation.3 | async-start | bytes 9437184 | tf_op jit(solution)/shard_map/all_gather | solution.py:8
Sparse Core Ops, SparseCore 0:
  66.9 124.0 all-gather.2
